TPU v7x, 512 devices: a whole 4x4x16 slice. The times are simulated.
512 devices in a mesh: rows: 128 (over y, z, core), users: 4 (over x).
Axes of the slice: x: 4, y: 4, z: 16, core: 2. Of those that a mesh axis runs over, the one named last changes fastest.
Arguments:
- old_basis: bfloat16 [49152, 4096], P('rows', 'users'), may hold values from -24 to 24
- new_atoms: bfloat16 [49152, 128], P('rows'), may hold values from -300 to 300
- user_residuals: bfloat16 [49152, 512], P('rows', 'users'), may hold values from -850 to 850
Outputs:
- new_block: bfloat16 [49152, 128], P('rows')
- updated_residuals: bfloat16 [49152, 512], P('rows', 'users')
All inputs are finite; a program needn't handle non-finite values.
Results may differ from a plain program's by a relative error of at most 0.019.
Values may be sent and summed in bfloat16 or wider, within the bound.
A program may use at most 64 MiB of HBM per device.

v0:
```python
import jax
import jax.numpy as jnp
from jax import lax
from jax.sharding import PartitionSpec as P


def coefficient_sum(partial_coef, m_total):
    summed = lax.psum(partial_coef, "rows")
    return (summed / m_total).astype(jnp.bfloat16)


def rows_product(left_rows, right_rows):
    return jnp.einsum("rk,rb->kb", left_rows, right_rows, preferred_element_type=jnp.float32)


def finish_block(remainder_low, gram_total, coupling_total, user_residuals, m_total):
    gram_matrix = gram_total / m_total
    factor_lower = jnp.linalg.cholesky(gram_matrix)
    identity = jnp.eye(gram_matrix.shape[0], dtype=jnp.float32)
    inverse = jax.scipy.linalg.solve_triangular(factor_lower, identity, lower=True)
    new_block = jnp.dot(
        remainder_low.astype(jnp.float32), inverse.T, precision=lax.Precision.HIGHEST
    ).astype(jnp.bfloat16)
    weights_low = jnp.dot(
        inverse, coupling_total / m_total, precision=lax.Precision.HIGHEST
    ).astype(jnp.bfloat16)
    updated = user_residuals.astype(jnp.float32) - jnp.dot(
        new_block, weights_low, preferred_element_type=jnp.float32
    )
    return (new_block, updated.astype(jnp.bfloat16))


def local(old_basis, new_atoms, user_residuals):
    local_rows = old_basis.shape[0]
    m_total = float(local_rows * lax.axis_size("rows"))
    remainder = new_atoms.astype(jnp.float32)
    remainder_low = new_atoms
    for sweep_index in range(2):
        coef_low = coefficient_sum(rows_product(old_basis, remainder_low), m_total)
        local_image = jnp.dot(old_basis, coef_low, preferred_element_type=jnp.float32)
        projected = lax.psum(local_image, "users")
        remainder = remainder - projected
        remainder_low = remainder.astype(jnp.bfloat16)
    gram_total, coupling_total = lax.psum(
        (rows_product(remainder_low, remainder_low), rows_product(remainder_low, user_residuals)),
        "rows",
    )
    return finish_block(remainder_low, gram_total, coupling_total, user_residuals, m_total)


def solution(mesh):
    in_specs = (P("rows", "users"), P("rows", None), P("rows", "users"))
    out_specs = (P("rows", None), P("rows", "users"))
    return jax.shard_map(local, mesh=mesh, in_specs=in_specs, out_specs=out_specs, check_vma=False)
```

profile of v0, /device:TPU:2, one launch (start us, length us, event | category | flops | bytes accessed | tf_op | source)
XLA Modules:
  0.0 1168.0 jit_solution(7656072023004440981)
XLA Ops:
  7.2 0.0 copy-start
  7.2 0.0 all-reduce.7.cloned.1.call-start
  7.2 1.1 copy-done
  8.3 2.1 fusion.14
  10.4 0.0 all-reduce.7.cloned.1.call-update
  10.4 0.0 all-reduce.9.cloned.1.call-start
  10.5 341.6 %all-reduce.7.cloned.1.call-done = f32[1024,128]{1,0:T(8,128)} async-done(((f32[1024,128]{1,0:T(8,128)}), f32[1024,128]{1,0:T(8,128)}) %all-reduce.7.cloned.1.call-update) | async-done | bytes 524304 | tf_op jit(solution)/shard_map/psum | solution.py:8
  352.1 2.1 convolution_bitcast_fusion.2
  354.2 0.0 copy-start.4
  354.2 0.0 all-reduce.9.cloned.1.call-update
  354.2 0.0 all-reduce.11.cloned.1.call-start
  354.2 0.8 copy-done.4
  355.0 0.1 copy.5
  355.2 52.1 %all-reduce.9.cloned.1.call-done = f32[384,128]{0,1:T(8,128)} async-done(((f32[384,128]{0,1:T(8,128)}), f32[384,128]{0,1:T(8,128)}) %all-reduce.9.cloned.1.call-update) | async-done | bytes 196624 | tf_op jit(solution)/shard_map/psum | solution.py:41
  407.3 2.2 convolution_bitcast_fusion
  409.5 0.0 all-reduce.11.cloned.1.call-update
  409.5 0.0 all-reduce.13.cloned.1.call-start
  409.5 338.9 %all-reduce.11.cloned.1.call-done = f32[1024,128]{1,0:T(8,128)} async-done(((f32[1024,128]{1,0:T(8,128)}), f32[1024,128]{1,0:T(8,128)}) %all-reduce.11.cloned.1.call-update) | async-done | bytes 524304 | tf_op jit(solution)/shard_map/psum | solution.py:8
  748.4 2.1 convolution_bitcast_fusion.1
  750.5 0.0 copy-start.1
  750.5 0.0 all-reduce.13.cloned.1.call-update
  750.5 0.0 all-reduce.15.cloned.1.call-start
  750.6 53.0 %all-reduce.13.cloned.1.call-done = f32[384,128]{0,1:T(8,128)} async-done(((f32[384,128]{0,1:T(8,128)}), f32[384,128]{0,1:T(8,128)}) %all-reduce.13.cloned.1.call-update) | async-done | bytes 196624 | tf_op jit(solution)/shard_map/psum | solution.py:41
  803.6 0.0 copy-done.1
  803.6 1.0 subtract_convert_fusion
  804.5 0.0 copy-start.2
  804.5 0.8 fusion.15
  805.3 0.1 copy-done.2
  805.4 0.9 fusion.16
  806.3 0.0 all-reduce.15.cloned.1.call-update
  806.3 328.4 %all-reduce.15.cloned.1.call-done = (f32[128,128]{0,1:T(8,128)}, f32[128,128]{0,1:T(8,128)}) async-done(((f32[128,128]{0,1:T(8,128)}, f32[128,128]{0,1:T(8,128)}), (f32[128,128]{0,1:T(8,128)}, f32[128,128]{0,1:T(8,128)})) %all-reduce.15.cloned.1.call-update) | async-done | bytes 131088 | tf_op jit(solution)/shard_map/psum | solution.py:44
  1134.7 0.8 broadcast_multiply_fusion
  1135.5 0.0 copy-start.5
  1135.5 0.1 copy.7
  1135.6 0.7 copy-done.5
  1136.4 11.7 %cholesky.17 = f32[128,128]{1,0:T(8,128)S(1)} custom-call(f32[128,128]{1,0:T(8,128)S(1)} %fusion.8), custom_call_target="Cholesky" | custom-call | tf_op jit(solution)/shard_map/jit(cholesky)/cholesky | solution.py:18
  1148.1 0.6 compare_reduce_fusion
  1148.8 0.7 fusion.5
  1149.4 9.8 custom-call.7
  1159.3 0.2 fusion.6
  1159.5 0.0 copy-start.6
  1159.5 0.3 convolution_convert_fusion
  1159.8 0.0 copy-start.3
  1159.8 0.5 copy-done.6
  1160.4 0.3 convolution_convert_fusion.1
  1160.6 0.8 fusion
  1161.4 0.0 copy-done.3
  (2 shorter events, 0.0 us)
Async XLA Ops:
  7.2 1.1 copy-start
  7.2 344.9 %all-reduce.7.cloned.1.call-start = ((), (), s32[]{:S(2)}) async-start(), calls=%async_computation | async-start | bytes 1048576 | tf_op jit(solution)/shard_map/psum | solution.py:8
  10.4 396.9 %all-reduce.9.cloned.1.call-start = ((), (), s32[]{:S(2)}) async-start(), calls=%async_computation.1 | async-start | bytes 393216 | tf_op jit(solution)/shard_map/psum | solution.py:41
  354.2 0.9 copy-start.4
  354.2 394.2 %all-reduce.11.cloned.1.call-start = ((), (), s32[]{:S(2)}) async-start(), calls=%async_computation.2 | async-start | bytes 1048576 | tf_op jit(solution)/shard_map/psum | solution.py:8
  409.5 394.1 %all-reduce.13.cloned.1.call-start = ((), (), s32[]{:S(2)}) async-start(), calls=%async_computation.3 | async-start | bytes 393216 | tf_op jit(solution)/shard_map/psum | solution.py:41
  750.5 53.1 %copy-start.1 = (f32[384,128]{0,1:T(8,128)S(1)}, f32[384,128]{0,1:T(8,128)}, u32[]{:S(2)}) copy-start(f32[384,128]{0,1:T(8,128)} %all-reduce.9.cloned.1.call-done) | copy-start | bytes 589828
  750.5 384.2 %all-reduce.15.cloned.1.call-start = ((), (), s32[]{:S(2)}) async-start(), calls=%async_computation.4 | async-start | bytes 262144 | tf_op jit(solution)/shard_map/psum | solution.py:44
  804.5 0.9 copy-start.2
  1135.5 0.8 copy-start.5
  1159.5 0.8 copy-start.6
  1159.8 1.6 copy-start.3
Sparse Core Ops, SparseCore 0:
  11.4 340.5 all-reduce.6
  354.4 52.8 all-reduce.8
  410.7 337.6 all-reduce.10
  750.6 52.8 all-reduce.12
  807.5 327.1 all-reduce.14
where the time goes:
time: 1170 us
  waiting for transfers between devices  1110 us (95%)
  other arithmetic  24.7 us (2%)
  between operations  13.9 us (1%)
    psum x2, waiting for transfers between devices, coefficient_sum(): summed = lax.psum(partial_coef, 'rows')  680 us
    psum x1, waiting for transfers between devices, local(): lax.psum((rows_product(remainder_low, remainder_low), rows_product(remain...  328 us
    psum x2, waiting for transfers between devices, local(): projected = lax.psum(local_image, 'users')  105 us
  transfers between devices with their start and end apart: 5, of which 5 were waited for; matrix products, arithmetic and copies ran while one was open for 0% of the time, Pallas kernels for 0%

commit v1 on v0

--- a/solution.py
+++ b/solution.py
@@ -38,7 +38,7 @@
     for sweep_index in range(2):
         coef_low = coefficient_sum(rows_product(old_basis, remainder_low), m_total)
         local_image = jnp.dot(old_basis, coef_low, preferred_element_type=jnp.float32)
-        projected = lax.psum(local_image, "users")
+        projected = jnp.sum(lax.all_gather(local_image, "users"), axis=0)
         remainder = remainder - projected
         remainder_low = remainder.astype(jnp.bfloat16)
     gram_total, coupling_total = lax.psum(

time: 1170 us -> 1080 us (0.923)
  waiting for transfers between devices: 1110 us -> 995 us
  blocking collectives: 0 us -> 28 us
    psum x2 -> x0, waiting for transfers between devices: 105 us -> none  [local(): projected = lax.psum(local_image, 'users')]
    all_gather x0 -> x2, blocking collectives: none -> 28 us  [local(): projected = jnp.sum(lax.all_gather(local_image, 'users'), axis=0)]
  transfers between devices with their start and end apart: 5 -> 3, of which waited for: 5 -> 3; matrix products, arithmetic and copies ran while one was open for 0% -> 0% of each run, Pallas kernels for 0% -> 0%
where the time goes in v1:
time: 1080 us
  waiting for transfers between devices  995 us (92%)
  blocking collectives  28 us (3%)
  other arithmetic  24.7 us (2%)
  between operations  13.9 us (1%)
    psum x2, waiting for transfers between devices, coefficient_sum(): summed = lax.psum(partial_coef, 'rows')  673 us
    psum x1, waiting for transfers between devices, local(): lax.psum((rows_product(remainder_low, remainder_low), rows_product(remain...  322 us
    all_gather x2, blocking collectives, local(): projected = jnp.sum(lax.all_gather(local_image, 'users'), axis=0)  28 us
  transfers between devices with their start and end apart: 3, of which 3 were waited for; matrix products, arithmetic and copies ran while one was open for 0% of the time, Pallas kernels for 0%

profile of v1, /device:TPU:2, one launch (start us, length us, event | category | flops | bytes accessed | tf_op | source)
XLA Modules:
  0.0 1075.5 jit_solution(16269930076162726520)
XLA Ops:
  7.2 0.0 copy-start
  7.2 0.0 all-reduce.5.cloned.1.call-start
  7.2 1.1 copy-done
  8.3 2.1 fusion.14
  10.4 0.0 copy-start.3
  10.4 0.0 all-reduce.5.cloned.1.call-update
  10.4 0.0 all-reduce.7.cloned.1.call-start
  10.5 0.8 copy-done.3
  11.3 0.1 copy.7
  11.4 340.5 %all-reduce.5.cloned.1.call-done = f32[1024,128]{1,0:T(8,128)} async-done(((f32[1024,128]{1,0:T(8,128)}), f32[1024,128]{1,0:T(8,128)}) %all-reduce.5.cloned.1.call-update) | async-done | bytes 524304 | tf_op jit(solution)/shard_map/psum | solution.py:8
  351.9 1.4 convolution_bitcast_fusion.2
  353.3 14.0 %all-gather = f32[1536,128]{0,1:T(8,128)S(1)} all-gather(f32[384,128]{0,1:T(8,128)S(1)} %convolution_bitcast_fusion.2), channel_id=2, replica_groups=mesh['rows'=128,'users'=4] {'users'}, dimensions={0}, use_global_device_ids=true | all-gather | bytes 983040 | tf_op jit(solution)/shard_map/all_gather | solution.py:41
  367.3 0.3 reshape.14
  367.6 0.5 reduce_sum.18
  368.1 1.3 convolution_bitcast_fusion
  369.3 0.0 all-reduce.7.cloned.1.call-update
  369.4 0.0 all-reduce.9.cloned.1.call-start
  369.4 332.3 %all-reduce.7.cloned.1.call-done = f32[1024,128]{1,0:T(8,128)} async-done(((f32[1024,128]{1,0:T(8,128)}), f32[1024,128]{1,0:T(8,128)}) %all-reduce.7.cloned.1.call-update) | async-done | bytes 524304 | tf_op jit(solution)/shard_map/psum | solution.py:8
  701.8 1.4 convolution_bitcast_fusion.1
  703.2 14.0 %all-gather.1 = f32[1536,128]{0,1:T(8,128)S(1)} all-gather(f32[384,128]{0,1:T(8,128)S(1)} %convolution_bitcast_fusion.1), channel_id=3, replica_groups=mesh['rows'=128,'users'=4] {'users'}, dimensions={0}, use_global_device_ids=true | all-gather | bytes 983040 | tf_op jit(solution)/shard_map/all_gather | solution.py:41
  717.2 0.3 reshape.15
  717.4 0.5 reduce_sum.19
  718.0 0.0 copy-start.1
  718.0 0.8 fusion.15
  718.8 0.1 copy-done.1
  718.9 0.9 fusion.16
  719.7 0.0 all-reduce.9.cloned.1.call-update
  719.7 322.5 %all-reduce.9.cloned.1.call-done = (f32[128,128]{0,1:T(8,128)}, f32[128,128]{0,1:T(8,128)}) async-done(((f32[128,128]{0,1:T(8,128)}, f32[128,128]{0,1:T(8,128)}), (f32[128,128]{0,1:T(8,128)}, f32[128,128]{0,1:T(8,128)})) %all-reduce.9.cloned.1.call-update) | async-done | bytes 131088 | tf_op jit(solution)/shard_map/psum | solution.py:44
  1042.2 0.8 broadcast_multiply_fusion
  1043.1 0.0 copy-start.4
  1043.1 0.1 copy.9
  1043.2 0.7 copy-done.4
  1043.9 11.7 %cholesky.17 = f32[128,128]{1,0:T(8,128)S(1)} custom-call(f32[128,128]{1,0:T(8,128)S(1)} %fusion.8), custom_call_target="Cholesky" | custom-call | tf_op jit(solution)/shard_map/jit(cholesky)/cholesky | solution.py:18
  1055.7 0.6 compare_reduce_fusion
  1056.3 0.7 fusion.5
  1057.0 9.8 custom-call.7
  1066.8 0.2 fusion.6
  1067.0 0.0 copy-start.5
  1067.0 0.3 convolution_convert_fusion
  1067.3 0.0 copy-start.2
  1067.4 0.5 copy-done.5
  1067.9 0.3 convolution_convert_fusion.1
  1068.1 0.8 fusion
  1069.0 0.0 copy-done.2
  (3 shorter events, 0.1 us)
Async XLA Ops:
  7.2 1.1 copy-start
  7.2 344.7 %all-reduce.5.cloned.1.call-start = ((), (), s32[]{:S(2)}) async-start(), calls=%async_computation | async-start | bytes 1048576 | tf_op jit(solution)/shard_map/psum | solution.py:8
  10.4 0.9 copy-start.3
  10.4 691.3 %all-reduce.7.cloned.1.call-start = ((), (), s32[]{:S(2)}) async-start(), calls=%async_computation.1 | async-start | bytes 1048576 | tf_op jit(solution)/shard_map/psum | solution.py:8
  369.4 672.9 %all-reduce.9.cloned.1.call-start = ((), (), s32[]{:S(2)}) async-start(), calls=%async_computation.2 | async-start | bytes 262144 | tf_op jit(solution)/shard_map/psum | solution.py:44
  718.0 0.9 copy-start.1
  1043.1 0.8 copy-start.4
  1067.0 0.8 copy-start.5
  1067.3 1.6 copy-start.2
Sparse Core Ops, SparseCore 0:
  11.4 340.4 all-reduce.4
  369.5 332.2 all-reduce.6
  719.9 322.3 all-reduce.8
